TPU v7x, 32 devices: a whole 2x2x4 slice. The times are simulated.
32 devices in a mesh: tile: 4 (over y, x), orient: 8 (over z, core).
Axes of the slice: x: 2, y: 2, z: 4, core: 2. Of those that a mesh axis runs over, the one named last changes fastest.
Arguments:
- micrograph_tiles: bfloat16 [8, 512, 512], P('tile'), as said below
- tile_offsets: int32 [8, 2], P('tile'), may hold values from 0 to 3584
- library: bfloat16 [32, 8, 128, 128], P('tile', 'orient'), as said below
- orient_ids: int32 [8, 2], P('orient'), may hold values from 0 to 31
Outputs:
- peak_score: float32 [8, 384, 384], P('tile')
- z_score: float32 [8, 384, 384], P('tile')
Inputs may be any that keep to these rules, and one draw needn't show every extreme that they name: `micrograph_tiles`: real-valued pixel intensities of the tiles. `library`: real-valued projection densities.
All inputs are finite; a program needn't handle non-finite values.
Results may differ from a plain program's by a relative error of at most 0.0095.
Values may be sent and summed in bfloat16 or wider, within the bound.
A program may use at most 64 MiB of HBM per device.

v0:
```python
import math

import jax
import jax.numpy as jnp
from jax import lax
from jax.sharding import PartitionSpec as P

VALID = 384
STEPS = 2


AMPLITUDE = 0.07
DEFOCUS_BASE = 100.0
DEFOCUS_TILT = 0.002
FLOOR_SHARE = 0.25


def from_root(value, axis, source):
    kept = jnp.where(lax.axis_index(axis) == source, value, 0).astype(value.dtype)
    return lax.psum(kept, axis)


def dft_tables(length):
    counter = jnp.arange(length, dtype=jnp.int32)
    product = counter[:, None] * counter[None, :] % length
    angle_table = product.astype(jnp.float32) * (2.0 * math.pi / length)
    return (jnp.cos(angle_table).astype(jnp.bfloat16), jnp.sin(angle_table).astype(jnp.bfloat16))


def frequency_squares(length):
    counter = jnp.arange(length, dtype=jnp.int32)
    signed = jnp.where(counter < length // 2, counter, counter - length)
    frequency = signed.astype(jnp.float32) / length
    return frequency[:, None] * frequency[:, None] + frequency[None, :] * frequency[None, :]


def batched(spec, left_op, right_op):
    return jnp.einsum(spec, left_op, right_op, preferred_element_type=jnp.float32)


def forward_tiles(images, cosine_table, sine_table):
    half_real = batched("tij,jk->tik", images, cosine_table).astype(jnp.bfloat16)
    half_imag = (-batched("tij,jk->tik", images, sine_table)).astype(jnp.bfloat16)
    spec_real = batched("ij,tjk->tik", cosine_table, half_real) + batched(
        "ij,tjk->tik", sine_table, half_imag
    )
    spec_imag = batched("ij,tjk->tik", cosine_table, half_imag) - batched(
        "ij,tjk->tik", sine_table, half_real
    )
    return (spec_real, spec_imag)


def tile_filters(tile_offsets, whiten, length):
    squares_freq = frequency_squares(length)
    offsets = tile_offsets.astype(jnp.float32)
    defocus = DEFOCUS_BASE + DEFOCUS_TILT * (offsets[:, 0] - offsets[:, 1])
    phase_angle = math.pi * defocus[:, None, None] * squares_freq[None]
    contrast = -(
        math.sqrt(1.0 - AMPLITUDE * AMPLITUDE) * jnp.sin(phase_angle)
        + AMPLITUDE * jnp.cos(phase_angle)
    )
    center = jnp.where(squares_freq > 0.0, 1.0, 0.0).astype(jnp.float32)
    return contrast * (whiten * center)[None]


def template_spectrum(template, cosine_table, sine_table):
    pattern_size = template.shape[0]
    tpl_real = jnp.dot(
        template, cosine_table[:pattern_size], preferred_element_type=jnp.float32
    ).astype(jnp.bfloat16)
    tpl_imag = (
        -jnp.dot(template, sine_table[:pattern_size], preferred_element_type=jnp.float32)
    ).astype(jnp.bfloat16)
    col_cos = cosine_table[:, :pattern_size]
    col_sin = sine_table[:, :pattern_size]
    base_real = jnp.dot(col_cos, tpl_real, preferred_element_type=jnp.float32) + jnp.dot(
        col_sin, tpl_imag, preferred_element_type=jnp.float32
    )
    base_imag = jnp.dot(col_cos, tpl_imag, preferred_element_type=jnp.float32) - jnp.dot(
        col_sin, tpl_real, preferred_element_type=jnp.float32
    )
    return (base_real, base_imag)


def correlate(
    base_real, base_imag, filters, white_real, white_imag, cosine_table, sine_table, valid_rows
):
    length = cosine_table.shape[0]
    filt_real = base_real[None] * filters
    filt_imag = base_imag[None] * filters
    energy = jnp.mean(filt_real * filt_real + filt_imag * filt_imag, axis=(1, 2), keepdims=True)
    norm_scale = lax.rsqrt(energy + 1e-06)
    norm_real = (filt_real * norm_scale).astype(jnp.bfloat16).astype(jnp.float32)
    norm_imag = (filt_imag * norm_scale).astype(jnp.bfloat16).astype(jnp.float32)
    wide_real = white_real.astype(jnp.float32)
    wide_imag = white_imag.astype(jnp.float32)
    prod_real = (wide_real * norm_real + wide_imag * norm_imag).astype(jnp.bfloat16)
    prod_imag = (wide_imag * norm_real - wide_real * norm_imag).astype(jnp.bfloat16)
    row_cos = cosine_table[:valid_rows]
    row_sin = sine_table[:valid_rows]
    mid_real = (
        batched("ij,tjk->tik", row_cos, prod_real) - batched("ij,tjk->tik", row_sin, prod_imag)
    ).astype(jnp.bfloat16)
    mid_imag = (
        batched("ij,tjk->tik", row_cos, prod_imag) + batched("ij,tjk->tik", row_sin, prod_real)
    ).astype(jnp.bfloat16)
    result = batched("tij,jk->tik", mid_real, cosine_table[:, :valid_rows]) - batched(
        "tij,jk->tik", mid_imag, sine_table[:, :valid_rows]
    )
    return result / length


def finish_scores(running_peak, running_sum, squares, searched):
    mean_score = running_sum / searched
    variance = squares / searched - mean_score * mean_score
    return (running_peak, (running_peak - mean_score) * lax.rsqrt(variance + 1e-06))


def body(micrograph_tiles, tile_offsets, library, orient_ids):
    length = micrograph_tiles.shape[1]
    tile_count = micrograph_tiles.shape[0]
    slot_count = library.shape[0]
    cosine_table, sine_table = dft_tables(length)
    spec_real, spec_imag = forward_tiles(micrograph_tiles, cosine_table, sine_table)
    local_power = jnp.sum(spec_real * spec_real + spec_imag * spec_imag, axis=0)
    mean_power = lax.psum(local_power, "tile") / (tile_count * lax.axis_size("tile"))
    whiten = lax.rsqrt(jnp.maximum(mean_power, FLOOR_SHARE * jnp.mean(mean_power)))
    white_real = (spec_real * whiten[None]).astype(jnp.bfloat16)
    white_imag = (spec_imag * whiten[None]).astype(jnp.bfloat16)
    filters = tile_filters(tile_offsets, whiten, length)
    running_peak = jnp.full((tile_count, VALID, VALID), -jnp.inf, jnp.float32)
    running_sum = jnp.zeros((tile_count, VALID, VALID), jnp.float32)
    squares = jnp.zeros((tile_count, VALID, VALID), jnp.float32)
    for step_index in range(STEPS):
        chosen = orient_ids[0, step_index]
        owner_index = chosen // slot_count
        slot_index = chosen % slot_count
        picked = lax.dynamic_index_in_dim(library[:, 0], slot_index, 0, keepdims=False)
        template = from_root(picked, "tile", owner_index)
        base_real, base_imag = template_spectrum(template, cosine_table, sine_table)
        scores = correlate(
            base_real, base_imag, filters, white_real, white_imag, cosine_table, sine_table, VALID
        )
        running_peak = jnp.maximum(running_peak, scores)
        running_sum = running_sum + scores
        squares = squares + scores * scores
    searched = STEPS * lax.axis_size("orient")
    total_peak = lax.pmax(running_peak, "orient")
    total_sum, total_squares = (
        lax.psum(running_sum.astype(jnp.bfloat16), "orient").astype(jnp.float32),
        lax.psum(squares.astype(jnp.bfloat16), "orient").astype(jnp.float32),
    )
    peak_score, z_score = finish_scores(total_peak, total_sum, total_squares, searched)
    return (peak_score, z_score)


def solution(mesh):
    placed = (
        P("tile", None, None),
        P("tile", None),
        P("tile", "orient", None, None),
        P("orient", None),
    )
    return jax.shard_map(
        body,
        mesh=mesh,
        in_specs=placed,
        out_specs=(P("tile", None, None), P("tile", None, None)),
        check_vma=False,
    )
```

profile of v0, /device:TPU:0, one launch (start us, length us, event | category | flops | bytes accessed | tf_op | source)
XLA Modules:
  0.0 309.6 jit_solution(17163099969103459368)
XLA Ops:
  15.3 5.5 %fusion.20 = bf16[2,512,512]{1,2,0:T(8,128)(2,1)S(1)} fusion(bf16[2,512,512]{2,1,0:T(8,128)(2,1)S(1)} %copy-done), kind=kOutput, calls=%fused_computation.57 | convolution fusion | flops 541851648 | bytes 2097152 | tf_op jit(solution)/shard_map/tij,jk->tik/dot_general | solution.py:38
  20.7 5.4 %fusion.19 = bf16[2,512,512]{1,2,0:T(8,128)(2,1)S(1)} fusion(bf16[2,512,512]{2,1,0:T(8,128)(2,1)S(1)} %copy-done), kind=kOutput, calls=%fused_computation.56 | convolution fusion | flops 541327360 | bytes 2097152 | tf_op jit(solution)/shard_map/tij,jk->tik/dot_general | solution.py:38
  26.2 5.6 %fusion.40 = f32[2,512,512]{2,1,0:T(8,128)S(1)} fusion(bf16[2,512,512]{1,2,0:T(8,128)(2,1)S(1)} %fusion.19), kind=kOutput, calls=%fused_computation.89 | convolution fusion | flops 540803072 | bytes 3145728 | tf_op jit(solution)/shard_map/ij,tjk->tik/dot_general | solution.py:38
  31.8 5.6 %fusion.38 = f32[2,512,512]{2,1,0:T(8,128)S(1)} fusion(bf16[2,512,512]{1,2,0:T(8,128)(2,1)S(1)} %fusion.20), kind=kOutput, calls=%fused_computation.87 | convolution fusion | flops 540803072 | bytes 3145728 | tf_op jit(solution)/shard_map/ij,tjk->tik/dot_general | solution.py:38
  37.4 6.1 %convolution_add_fusion = f32[2,512,512]{2,1,0:T(8,128)S(1)} fusion(f32[2,512,512]{2,1,0:T(8,128)S(1)} %fusion.40, bf16[2,512,512]{1,2,0:T(8,128)(2,1)S(1)} %fusion.20), kind=kOutput, calls=%fused_computation.39 | convolution fusion | flops 541327360 | bytes 5242880 | tf_op jit(solution)/shard_map/ij,tjk->tik/dot_general | solution.py:38
  43.5 7.5 %fusion.14 = (f32[512,512]{0,1:T(8,128)}, f32[2,512,512]{2,1,0:T(8,128)}) fusion(f32[2,512,512]{2,1,0:T(8,128)S(1)} %convolution_add_fusion, f32[2,512,512]{2,1,0:T(8,128)S(1)} %fusion.38, bf16[2,512,512]{1,2,0:T(8,128)(2,1)S(1)} %fusion.19), kind=kOutput, calls=%fused_computation.26 | convolution fusion | flops 543162368 | bytes 8388608 | tf_op jit(solution)/shard_map/ij,tjk->tik/dot_general | solution.py:38
  51.2 3.9 %cosine_convert_fusion = bf16[512,512]{1,0:T(8,128)(2,1)S(1)} fusion(), kind=kLoop, calls=%fused_computation.79 | loop fusion | flops 3932160 | bytes 524288 | tf_op jit(solution)/shard_map/convert_element_type | solution.py:27
  55.1 4.0 %sine_convert_fusion = bf16[512,512]{1,0:T(8,128)(2,1)S(1)} fusion(), kind=kLoop, calls=%fused_computation.78 | loop fusion | flops 3932160 | bytes 524288 | tf_op jit(solution)/shard_map/convert_element_type | solution.py:27
  59.3 3.9 %all-reduce.13.cloned.1.call-done = (bf16[128,128]{1,0:T(8,128)(2,1)}, bf16[128,128]{1,0:T(8,128)(2,1)}) async-done(((bf16[128,128]{1,0:T(8,128)(2,1)}, bf16[128,128]{1,0:T(8,128)(2,1)}), (bf16[128,128]{1,0:T(8,128)(2,1)}, bf16[128,128]{1,0:T(8,128)(2,1)})) %all-reduce.13.cloned.1.call-update) | async-done | bytes 65552 | tf_op jit(solution)/shard_map/psum | solution.py:20
  70.4 3.0 convolution_add_fusion.2
  73.4 2.6 copy.8
  77.7 2.5 copy.11
  81.8 2.6 copy.10
  84.4 34.4 %all-reduce.7.cloned.1.call-done = f32[512,512]{0,1:T(8,128)} async-done(((f32[512,512]{0,1:T(8,128)}), f32[512,512]{0,1:T(8,128)}) %all-reduce.7.cloned.1.call-update) | async-done | bytes 1048592 | tf_op jit(solution)/shard_map/psum | solution.py:126
  123.7 9.8 %add_reduce_fusion = (f32[2]{0:T(128)S(1)}, f32[2]{0:T(128)S(1)}) fusion(f32[512,512]{0,1:T(8,128)S(1)} %copy-done.5, f32[512,512]{0,1:T(8,128)S(1)} %copy-done.6, f32[512,512]{0,1:T(8,128)S(1)} %get-tuple-element.16, f32[512,512]{0,1:T(8,128)S(1)} %get-tuple-element.24, f32[2]{0:T(128)S(1)} %multiply_reduce_fusion.1, f32[512,512]{0,1:T(8,128)S(1)} %copy.9, ...), kind=kLoop, calls=%fused_computation.33 | loop fusion | flops 9437180 | bytes 6291480 | tf_op jit(solution)/shard_map/reduce_sum | solution.py:91
  133.6 9.8 %fusion.12 = (bf16[2,512,512]{1,2,0:T(8,128)(2,1)}, bf16[2,512,512]{1,2,0:T(8,128)(2,1)S(1)}, bf16[2,512,512]{1,2,0:T(8,128)(2,1)S(1)}, bf16[2,512,512]{1,2,0:T(8,128)(2,1)S(1)}, bf16[2,512,512]{1,2,0:T(8,128)(2,1)S(1)}) fusion(f32[2]{0:T(128)S(1)} %get-tuple-element.30, f32[512,512]{0,1:T(8,128)S(1)} %get-tuple-element.16, ...), kind=kLoop, calls=%fused_computation.22 | loop fusion | flops 12582912 | bytes 14680080 | tf_op jit(solution)/shard_map/convert_element_type | solution.py:98
  143.4 9.5 %fusion.8 = (bf16[2,512,512]{1,2,0:T(8,128)(2,1)S(1)}, bf16[2,512,512]{1,2,0:T(8,128)(2,1)S(1)}, bf16[2,512,512]{1,2,0:T(8,128)(2,1)S(1)}, bf16[2,512,512]{1,2,0:T(8,128)(2,1)S(1)}) fusion(bf16[2,512,512]{1,2,0:T(8,128)(2,1)S(1)} %get-tuple-element.12, bf16[2,512,512]{1,2,0:T(8,128)(2,1)S(1)} %get-tuple-element.11, f32[2]{0:T(128)S(1)} %get-tuple-element.31, ...), kind=kLoop, calls=%fused_computation.18 | loop fusion | flops 13631488 | bytes 12582928 | tf_op jit(solution)/shard_map/convert_element_type | solution.py:98
  158.1 3.8 %fusion.26 = f32[2,384,384]{2,1,0:T(8,128)} fusion(f32[2,512,384]{1,2,0:T(8,128)} %fusion.50, bf16[2,512,512]{1,2,0:T(8,128)(2,1)} %copy-done.8, bf16[512,512]{1,0:T(8,128)(2,1)S(1)} %cosine_convert_fusion, bf16[512,512]{1,0:T(8,128)(2,1)S(1)} %sine_convert_fusion), kind=kOutput, calls=%fused_computation.63 | convolution fusion | flops 705429504 | bytes 4587520 | tf_op jit(solution)/shard_map/tij,jk->tik/dot_general | solution.py:38
  165.4 3.8 %fusion.25 = f32[2,384,384]{2,1,0:T(8,128)} fusion(f32[2,512,384]{1,2,0:T(8,128)} %fusion.48, bf16[2,512,512]{1,2,0:T(8,128)(2,1)} %get-tuple-element.8, bf16[512,512]{1,0:T(8,128)(2,1)S(1)} %cosine_convert_fusion, bf16[512,512]{1,0:T(8,128)(2,1)S(1)} %sine_convert_fusion), kind=kOutput, calls=%fused_computation.62 | convolution fusion | flops 705429504 | bytes 4587520 | tf_op jit(solution)/shard_map/tij,jk->tik/dot_general | solution.py:38
  169.1 3.8 %fusion.17 = f32[2,384,384]{2,1,0:T(8,128)} fusion(f32[2,384,384]{2,1,0:T(8,128)} %fusion.25, f32[2,512,384]{1,2,0:T(8,128)} %fusion.47, bf16[2,512,512]{1,2,0:T(8,128)(2,1)S(1)} %get-tuple-element.21, bf16[512,512]{1,0:T(8,128)(2,1)S(1)} %sine_convert_fusion), kind=kOutput, calls=%fused_computation.49 | convolution fusion | flops 706019328 | bytes 5767168 | tf_op jit(solution)/shard_map/tij,jk->tik/dot_general | solution.py:38
  172.9 4.9 %add_convert_fusion.3 = (bf16[2,384,384]{2,1,0:T(8,128)(2,1)}, bf16[2,384,384]{2,1,0:T(8,128)(2,1)}, f32[2,384,384]{2,1,0:T(8,128)}) fusion(f32[2,384,384]{2,1,0:T(8,128)} %fusion.17, f32[2,384,384]{2,1,0:T(8,128)} %fusion.26, bf16[512,512]{1,0:T(8,128)(2,1)S(1)} %sine_convert_fusion, f32[2,512,384]{1,2,0:T(8,128)} %fusion.49, ...), kind=kOutput, calls=%fused_computation.66 | convolution fusion | flops 708083712 | bytes 8126464 | tf_op jit(solution)/shard_map/tij,jk->tik/dot_general | solution.py:38
  178.4 59.4 %all-reduce.9.cloned.1.call-done = f32[2,384,384]{2,1,0:T(8,128)} async-done(((f32[2,384,384]{2,1,0:T(8,128)}), f32[2,384,384]{2,1,0:T(8,128)}) %all-reduce.9.cloned.1.call-update) | async-done | bytes 1179664 | tf_op jit(solution)/shard_map/pmax | solution.py:148
  237.8 61.2 %all-reduce.11.cloned.1.call-done = (bf16[2,384,384]{2,1,0:T(8,128)(2,1)}, bf16[2,384,384]{2,1,0:T(8,128)(2,1)}) async-done(((bf16[2,384,384]{2,1,0:T(8,128)(2,1)}, bf16[2,384,384]{2,1,0:T(8,128)(2,1)}), (bf16[2,384,384]{2,1,0:T(8,128)(2,1)}, bf16[2,384,384]{2,1,0:T(8,128)(2,1)})) %all-reduce.11.cloned.1.call-update) | async-done | bytes 1179664 | tf_op jit(solution)/shard_map/psum | solution.py:151
  299.0 3.0 rsqrt_multiply_fusion
  (64 shorter events, 28.2 us)
Async XLA Ops:
  7.2 8.1 %copy-start = (bf16[2,512,512]{2,1,0:T(8,128)(2,1)S(1)}, bf16[2,512,512]{2,1,0:T(8,128)(2,1)}, u32[]{:S(2)}) copy-start(bf16[2,512,512]{2,1,0:T(8,128)(2,1)} %param.4) | copy-start | bytes 3145732
  7.2 56.0 %all-reduce.13.cloned.1.call-start = ((), (), s32[]{:S(2)}) async-start(), calls=%async_computation.3 | async-start | bytes 131072 | tf_op jit(solution)/shard_map/psum | solution.py:20
  15.2 103.6 %all-reduce.7.cloned.1.call-start = ((), (), s32[]{:S(2)}) async-start(), calls=%async_computation | async-start | bytes 2097152 | tf_op jit(solution)/shard_map/psum | solution.py:126
  43.5 7.5 %copy-start.10 = (f32[2,512,512]{2,1,0:T(8,128)}, f32[2,512,512]{2,1,0:T(8,128)S(1)}, u32[]{:S(2)}) copy-start(f32[2,512,512]{2,1,0:T(8,128)S(1)} %convolution_add_fusion) | copy-start | bytes 6291460
  50.9 8.2 %copy-start.14 = (s32[2,2]{1,0:T(2,128)S(1)}, s32[2,2]{1,0:T(2,128)}, u32[]{:S(2)}) copy-start(s32[2,2]{1,0:T(2,128)} %param.5) | copy-start | bytes 52
  50.9 186.9 %all-reduce.9.cloned.1.call-start = ((), (), s32[]{:S(2)}) async-start(), calls=%async_computation.1 | async-start | bytes 2359296 | tf_op jit(solution)/shard_map/pmax | solution.py:148
  70.4 52.9 %copy-start.1 = (f32[512,512]{0,1:T(8,128)}, f32[512,512]{0,1:T(8,128)S(1)}, u32[]{:S(2)}) copy-start(f32[512,512]{0,1:T(8,128)S(1)} %copy.9) | copy-start | bytes 3145732
  73.4 2.9 copy-start.13
  121.6 1.7 copy-start.3
  121.6 1.8 copy-start.5
  121.6 2.2 copy-start.6
  123.7 9.8 %copy-start.11 = (f32[2,512,512]{2,1,0:T(8,128)S(1)}, f32[2,512,512]{2,1,0:T(8,128)}, u32[]{:S(2)}) copy-start(f32[2,512,512]{2,1,0:T(8,128)} %copy-done.10) | copy-start | bytes 6291460
  123.7 9.8 %copy-start.12 = (f32[2,512,512]{2,1,0:T(8,128)S(1)}, f32[2,512,512]{2,1,0:T(8,128)}, u32[]{:S(2)}) copy-start(f32[2,512,512]{2,1,0:T(8,128)} %get-tuple-element.28) | copy-start | bytes 6291460
  133.6 9.8 %copy-start.2 = (f32[512,512]{0,1:T(8,128)S(1)}, f32[512,512]{0,1:T(8,128)}, u32[]{:S(2)}) copy-start(f32[512,512]{0,1:T(8,128)} %copy-done.1) | copy-start | bytes 3145732
  152.9 3.4 %copy-start.8 = (bf16[2,512,512]{1,2,0:T(8,128)(2,1)}, bf16[2,512,512]{1,2,0:T(8,128)(2,1)S(1)}, u32[]{:S(2)}) copy-start(bf16[2,512,512]{1,2,0:T(8,128)(2,1)S(1)} %get-tuple-element.13) | copy-start | bytes 3145732
  153.6 1.0 copy-start.4
  161.8 1.8 copy-start.9
  177.9 121.2 %all-reduce.11.cloned.1.call-start = ((), (), s32[]{:S(2)}) async-start(), calls=%async_computation.2 | async-start | bytes 2359296 | tf_op jit(solution)/shard_map/psum | solution.py:151
  237.8 64.2 %copy-start.7 = (f32[2,384,384]{2,1,0:T(8,128)S(1)}, f32[2,384,384]{2,1,0:T(8,128)}, u32[]{:S(2)}) copy-start(f32[2,384,384]{2,1,0:T(8,128)} %all-reduce.9.cloned.1.call-done) | copy-start | bytes 3538948
Sparse Core Ops, SparseCore 0:
  15.3 47.8 all-reduce.12
  66.3 52.4 all-reduce.6
  178.0 59.8 all-reduce.8
  240.1 58.8 all-reduce.10
where the time goes:
time: 310 us
  waiting for transfers between devices  159 us (51%)
  matrix products  70.7 us (23%)
  other arithmetic  46 us (15%)
  between operations  19.9 us (6%)
  local copies, waits for them, and re-layouts  13.2 us (4%)
    psum x1, waiting for transfers between devices, body(): lax.psum(squares.astype(jnp.bfloat16), 'orient').astype(jnp.float32)  61.2 us
    pmax x1, waiting for transfers between devices, body(): total_peak = lax.pmax(running_peak, 'orient')  59.4 us
    dot_general x14, matrix products, batched(): jnp.einsum(spec, left_op, right_op, preferred_element_type=jnp.float32)  58.8 us
    psum x1, waiting for transfers between devices, body(): lax.psum(local_power, 'tile') / (tile_count * lax.axis_size('tile'))  34.4 us
    convert_element_type x2, other arithmetic, correlate(): (wide_imag * norm_real - wide_real * norm_imag).astype(jnp.bfloat16)  19.3 us
    reduce_sum x1, other arithmetic, correlate(): jnp.mean(filt_real * filt_real + filt_imag * filt_imag, axis=(1, 2), keep...  9.79 us
  transfers between devices with their start and end apart: 4, of which 4 were waited for; matrix products, arithmetic and copies ran while one was open for 21% of the time, Pallas kernels for 0%

commit v1 on v0

v1 whole, which is shorter than its diff:
```python
import functools
import math

import jax
import jax.numpy as jnp
import numpy as np
from jax import lax
from jax.experimental import pallas as pl
from jax.experimental.pallas import tpu as pltpu
from jax.sharding import PartitionSpec as P

VALID = 384

AMPLITUDE = 0.07
DEFOCUS_BASE = 100.0
DEFOCUS_TILT = 0.002
FLOOR_SHARE = 0.25
MESH = pl.DeviceIdType.MESH
VMEM = pl.BlockSpec(memory_space=pltpu.VMEM)
SMEM = pl.BlockSpec(memory_space=pltpu.SMEM)
GRANT = 56 * 1024 * 1024


def tables(length, valid):
    half = length // 2
    rows = -(-(half + 1) // 16) * 16
    a_index = np.concatenate([np.arange(0, length, 2), np.arange(1, length, 2)])
    j_index = np.arange(length)
    b_index = np.arange(half + 1)

    def wave(function, left, right):
        return function((left[:, None] * right[None, :]) % length * (2.0 * np.pi / length))

    first = np.zeros((2, rows, length))
    first[0, : half + 1] = wave(np.cos, b_index, j_index)
    first[1, : half + 1] = -wave(np.sin, b_index, j_index)
    second_cos = wave(np.cos, j_index, a_index)
    second_sin = wave(np.sin, j_index, a_index)
    back = []
    for parity in range(2):
        cosine = wave(np.cos, a_index[parity * half : (parity + 1) * half], j_index[:half])
        sine = wave(np.sin, a_index[parity * half : (parity + 1) * half], j_index[:half])
        back.append(np.block([[cosine, sine], [-sine, cosine]]))
    count = np.full((half,), 2.0)
    count[0] = 1.0
    last_cos = wave(np.cos, j_index[:valid], b_index[:half]) * count / length
    last_sin = -wave(np.sin, j_index[:valid], b_index[:half]) * count / length
    last_sin[:, 0] = np.cos(np.pi * j_index[:valid]) / length
    last = np.concatenate([last_cos, last_sin], axis=1)

    signed = np.where(a_index < half, a_index, a_index - length) / length
    a_square = (signed * signed)[None, :]
    b_square = np.zeros((rows, 1))
    b_square[: half + 1, 0] = (b_index / length) ** 2
    weight = np.zeros((rows, 1))
    weight[: half + 1, 0] = 2.0
    weight[0, 0] = weight[half, 0] = 1.0

    def narrow(value):
        return np.asarray(value, np.float32).astype(jnp.bfloat16)

    return dict(
        first=narrow(first.reshape(2 * rows, length)),
        cos=narrow(second_cos),
        sin=narrow(second_sin),
        even=narrow(back[0]),
        odd=narrow(back[1]),
        last=narrow(last),
        a_square=a_square.astype(np.float32),
        b_square=b_square.astype(np.float32),
        weight=weight.astype(np.float32),
    )


def dot(left, right):
    return jnp.dot(left, right, preferred_element_type=jnp.float32)


def dot_nt(left, right):
    return lax.dot_general(
        left, right, (((1,), (1,)), ((), ())), preferred_element_type=jnp.float32
    )


def sine_of_turns(turns):
    part = turns - jnp.floor(turns + 0.5)
    mirrored = jnp.where(part > 0.0, 0.5, -0.5) - part
    part = jnp.where(jnp.abs(part) > 0.25, mirrored, part)
    angle = part * (2.0 * math.pi)
    square = angle * angle
    poly = -1.0 / 39916800.0
    for term in (1.0 / 362880.0, -1.0 / 5040.0, 1.0 / 120.0, -1.0 / 6.0, 1.0):
        poly = poly * square + term
    return angle * poly


def forward_kernel(
    ids_ref, off_ref, x_ref, lib_ref, first_ref, cos_ref, sin_ref, a_ref, b_ref,
    real_ref, imag_ref, con_ref, pow_ref, tpl_ref,
):
    core = lax.rem(lax.axis_index("orient"), 2)
    mine = lax.axis_index("tile")
    slots = lib_ref.shape[0]
    rows, length = real_ref.shape
    half = length // 2
    for step in range(tpl_ref.shape[0]):
        chosen = ids_ref[0, step]
        owner = chosen // slots
        picked = lib_ref[chosen - owner * slots, 0]
        keep = jnp.where(owner == mine, 1.0, 0.0).astype(jnp.float32)
        tpl_ref[step] = jnp.where(keep > 0.0, picked.astype(jnp.float32), 0.0).astype(jnp.bfloat16)
    halves = dot_nt(first_ref[...], x_ref[core]).astype(jnp.bfloat16)
    half_real, half_imag = halves[:rows], halves[rows:]
    spec_real = dot(half_real, cos_ref[...]) + dot(half_imag, sin_ref[...])
    spec_imag = dot(half_imag, cos_ref[...]) - dot(half_real, sin_ref[...])
    power = spec_real * spec_real + spec_imag * spec_imag
    pow_ref[0] = power[:, :half].astype(jnp.bfloat16)
    pow_ref[1] = power[:, half:].astype(jnp.bfloat16)
    s2 = a_ref[...] + b_ref[...]
    tilt = (off_ref[core, 0] - off_ref[core, 1]).astype(jnp.float32)
    defocus = DEFOCUS_BASE + DEFOCUS_TILT * tilt
    shift = math.asin(AMPLITUDE) / (2.0 * math.pi)
    contrast = -sine_of_turns(s2 * (0.5 * defocus) + shift)
    contrast = jnp.where(s2 > 0.0, contrast, 0.0)
    con_ref[...] = contrast
    real_ref[...] = spec_real * contrast
    imag_ref[...] = spec_imag * contrast


def exchange_kernel(
    n_tile, n_orient, pow_ref, tpl_ref, total_ref, all_ref,
    pair_in, half_out, half_in, done_out, done_in, tpl_in, held, send_sem, recv_sem,
):
    tile = lax.axis_index("tile")
    orient = lax.axis_index("orient")
    core = lax.rem(orient, 2)
    chip = orient // 2
    n_chip = n_orient // 2
    partner = (tile, chip * 2 + 1 - core)
    tiles = [(lax.rem(tile + k, n_tile), orient) for k in range(1, n_tile)]
    chips = [(tile, lax.rem(chip + k, n_chip) * 2 + core) for k in range(1, n_chip)]

    barrier = pltpu.get_barrier_semaphore()
    for device in [partner] + tiles + chips:
        pl.semaphore_signal(barrier, inc=1, device_id=device, device_id_type=MESH)
    pl.semaphore_wait(barrier, 1 + len(tiles) + len(chips))

    used = [0]

    def send(src, dst, device):
        at = used[0]
        used[0] += 1
        copy = pltpu.make_async_remote_copy(
            src_ref=src, dst_ref=dst, send_sem=send_sem.at[at], recv_sem=recv_sem.at[at],
            device_id=device, device_id_type=MESH,
        )
        copy.start()
        return copy

    pair = send(pow_ref.at[1 - core], pair_in, partner)
    picks = [send(tpl_ref, tpl_in.at[k], device) for k, device in enumerate(tiles)]
    pair.wait()
    mine = pow_ref[core].astype(jnp.float32) + pair_in[...].astype(jnp.float32)
    half_out[...] = mine.astype(jnp.bfloat16)
    sums = [send(half_out, half_in.at[k], device) for k, device in enumerate(tiles)]
    template = tpl_ref[...].astype(jnp.float32)
    for k, copy in enumerate(picks):
        copy.wait()
        template = template + tpl_in[k].astype(jnp.float32)
    held[core, chip] = template.astype(jnp.bfloat16)
    spread = [send(held.at[core, chip], held.at[core, chip], device) for device in chips]
    for copy in sums:
        copy.wait()
    total = half_out[...].astype(jnp.float32)
    for k in range(len(tiles)):
        total = total + half_in[k].astype(jnp.float32)
    done_out[...] = total
    last = send(done_out, done_in, partner)
    for copy in spread:
        copy.wait()
    swap = send(held.at[core], held.at[core], partner)
    total_ref[core] = total
    last.wait()
    total_ref[1 - core] = done_in[...]
    swap.wait()
    all_ref[...] = held[...]


def search_kernel(
    tiles, real_ref, imag_ref, con_ref, total_ref, tpl_ref, first_ref, cos_ref, sin_ref,
    even_ref, odd_ref, last_ref, weight_ref, out_ref,
    g_real, g_imag, g_energy, base_table, mids, peak, total_sum, squares,
):
    rows, length = real_ref.shape
    half = length // 2
    valid = last_ref.shape[0]
    groups, steps, size, _ = tpl_ref.shape
    weight = weight_ref[...]
    sides = [total_ref[side] / tiles for side in range(2)]
    mean = (jnp.sum(sides[0] * weight) + jnp.sum(sides[1] * weight)) / (length * length)
    floor = FLOOR_SHARE * mean
    for side in range(2):
        columns = slice(side * half, (side + 1) * half)
        whiten2 = 1.0 / jnp.maximum(sides[side], floor)
        contrast = con_ref[:, columns]
        g_real[:, columns] = real_ref[:, columns] * whiten2
        g_imag[:, columns] = imag_ref[:, columns] * whiten2
        g_energy[:, columns] = contrast * contrast * whiten2 * (weight / (length * length))
    base_table[:size, :length] = cos_ref[:size]
    base_table[:size, length:] = -sin_ref[:size]
    base_table[size:, :length] = sin_ref[:size]
    base_table[size:, length:] = cos_ref[:size]
    peak[...] = jnp.full_like(peak, -jnp.inf)
    total_sum[...] = jnp.zeros_like(total_sum)
    squares[...] = jnp.zeros_like(squares)

    def visit(group, carry):
        images = tpl_ref[group].reshape(steps * size, size)
        halves = dot_nt(first_ref[...], images).astype(jnp.bfloat16)
        scales = []
        for step in range(steps):
            columns = slice(step * size, (step + 1) * size)
            joined = jnp.concatenate([halves[:rows, columns], halves[rows:, columns]], axis=1)
            base = dot(joined, base_table[...])
            base_real, base_imag = base[:, :length], base[:, length:]
            energy = jnp.sum(g_energy[...] * (base_real * base_real + base_imag * base_imag))
            scales.append(lax.rsqrt(energy + 1e-06))
            prod_real = (g_real[...] * base_real + g_imag[...] * base_imag).astype(jnp.bfloat16)
            prod_imag = (g_imag[...] * base_real - g_real[...] * base_imag).astype(jnp.bfloat16)
            even = dot(
                jnp.concatenate([prod_real[:, :half], prod_imag[:, :half]], axis=1), even_ref[...]
            )
            odd = dot(
                jnp.concatenate([prod_real[:, half:], prod_imag[:, half:]], axis=1), odd_ref[...]
            )
            both, apart = even + odd, even - odd
            mid_real = jnp.concatenate([both[:, :half], apart[:, : valid - half]], axis=1)
            mid_imag = jnp.concatenate([both[:half, half:], apart[:half, half:valid]], axis=1)
            row = lax.broadcasted_iota(jnp.int32, (half, valid), 0)
            mid_imag = jnp.where(row == 0, mid_real[half : half + 1], mid_imag)
            place = slice(step * valid, (step + 1) * valid)
            mids[:half, place] = mid_real[:half].astype(jnp.bfloat16)
            mids[half:, place] = mid_imag.astype(jnp.bfloat16)
        found = dot(last_ref[...], mids[...])
        top, add, add2 = peak[...], total_sum[...], squares[...]
        for step in range(steps):
            score = found[:, step * valid : (step + 1) * valid] * scales[step]
            top = jnp.maximum(top, score)
            add = add + score
            add2 = add2 + score * score
        peak[...] = top
        total_sum[...] = add
        squares[...] = add2
        return carry

    lax.fori_loop(0, groups, visit, 0)
    searched = groups * steps
    mean_score = total_sum[...] / searched
    variance = squares[...] / searched - mean_score * mean_score
    z_score = (peak[...] - mean_score) * lax.rsqrt(variance + 1e-06)
    out_ref[0] = peak[...].T.astype(jnp.bfloat16)
    out_ref[1] = z_score.T.astype(jnp.bfloat16)


def swap_kernel(in_ref, out_ref, held, send_sem, recv_sem):
    tile = lax.axis_index("tile")
    orient = lax.axis_index("orient")
    core = lax.rem(orient, 2)
    partner = (tile, (orient // 2) * 2 + 1 - core)
    barrier = pltpu.get_barrier_semaphore()
    pl.semaphore_signal(barrier, inc=1, device_id=partner, device_id_type=MESH)
    pl.semaphore_wait(barrier, 1)
    copy = pltpu.make_async_remote_copy(
        src_ref=in_ref, dst_ref=held, send_sem=send_sem, recv_sem=recv_sem,
        device_id=partner, device_id_type=MESH,
    )
    copy.start()
    for which in range(2):
        out_ref[which, core] = in_ref[which]
    copy.wait()
    for which in range(2):
        out_ref[which, 1 - core] = held[which]


def body(n_tile, n_orient, micrograph_tiles, tile_offsets, library, orient_ids):
    tile_count, length = micrograph_tiles.shape[:2]
    slots, _, size, _ = library.shape
    steps = orient_ids.shape[1]
    n_chip = n_orient // 2
    assert tile_count == 2 and n_orient % 2 == 0
    half = length // 2
    t = tables(length, VALID)
    rows = t["weight"].shape[0]
    f32, bf16 = jnp.float32, jnp.bfloat16
    shape = jax.ShapeDtypeStruct
    plane = shape((rows, length), f32)
    params = pltpu.CompilerParams(vmem_limit_bytes=GRANT)

    real, imag, contrast, power, picked = pl.pallas_call(
        forward_kernel,
        out_shape=(plane, plane, plane, shape((2, rows, half), bf16), shape((steps, size, size), bf16)),
        in_specs=[SMEM, SMEM] + [VMEM] * 7,
        out_specs=(VMEM,) * 5,
        compiler_params=params,
    )(
        orient_ids, tile_offsets, micrograph_tiles, library, t["first"], t["cos"], t["sin"],
        t["a_square"], t["b_square"],
    )

    copies = 3 + 2 * (n_tile - 1) + (n_chip - 1)
    total, templates = pl.pallas_call(
        functools.partial(exchange_kernel, n_tile, n_orient),
        out_shape=(shape((2, rows, half), f32), shape((2, n_chip, steps, size, size), bf16)),
        in_specs=[VMEM] * 2,
        out_specs=(VMEM,) * 2,
        scratch_shapes=[
            pltpu.VMEM((rows, half), bf16),
            pltpu.VMEM((rows, half), bf16),
            pltpu.VMEM((n_tile - 1, rows, half), bf16),
            pltpu.VMEM((rows, half), f32),
            pltpu.VMEM((rows, half), f32),
            pltpu.VMEM((n_tile - 1, steps, size, size), bf16),
            pltpu.VMEM((2, n_chip, steps, size, size), bf16),
            pltpu.SemaphoreType.DMA((copies,)),
            pltpu.SemaphoreType.DMA((copies,)),
        ],
        compiler_params=pltpu.CompilerParams(collective_id=0, has_side_effects=True),
    )(power, picked)

    found = pl.pallas_call(
        functools.partial(search_kernel, tile_count * n_tile),
        out_shape=shape((2, VALID, VALID), bf16),
        in_specs=[VMEM] * 12,
        out_specs=VMEM,
        scratch_shapes=[
            pltpu.VMEM((rows, length), f32),
            pltpu.VMEM((rows, length), f32),
            pltpu.VMEM((rows, length), f32),
            pltpu.VMEM((2 * size, 2 * length), bf16),
            pltpu.VMEM((length, steps * VALID), bf16),
            pltpu.VMEM((VALID, VALID), f32),
            pltpu.VMEM((VALID, VALID), f32),
            pltpu.VMEM((VALID, VALID), f32),
        ],
        compiler_params=params,
    )(
        real, imag, contrast, total, templates.reshape(n_orient, steps, size, size),
        np.ascontiguousarray(t["first"][:, :size]), t["cos"], t["sin"], t["even"], t["odd"],
        t["last"], t["weight"],
    )

    both = pl.pallas_call(
        swap_kernel,
        out_shape=shape((2, 2, VALID, VALID), bf16),
        in_specs=[VMEM],
        out_specs=VMEM,
        scratch_shapes=[
            pltpu.VMEM((2, VALID, VALID), bf16),
            pltpu.SemaphoreType.DMA,
            pltpu.SemaphoreType.DMA,
        ],
        compiler_params=pltpu.CompilerParams(collective_id=1, has_side_effects=True),
    )(found)
    return (both[0].astype(f32), both[1].astype(f32))


def solution(mesh):
    placed = (
        P("tile", None, None),
        P("tile", None),
        P("tile", "orient", None, None),
        P("orient", None),
    )
    return jax.shard_map(
        functools.partial(body, mesh.shape["tile"], mesh.shape["orient"]),
        mesh=mesh,
        in_specs=placed,
        out_specs=(P("tile", None, None), P("tile", None, None)),
        check_vma=False,
    )
```

time: 310 us -> 51.8 us (0.17)
  waiting for transfers between devices: 159 us -> 0 us
  matrix products: 70.7 us -> 0 us
  Pallas kernels: 0 us -> 48.1 us
  other arithmetic: 46 us -> 2.8 us
  between operations: 19.9 us -> 0.65 us
  local copies, waits for them, and re-layouts: 13.2 us -> 0 us
    psum x3 -> x0, waiting for transfers between devices: 99.5 us -> none  [the longest x1 61.2 us: body(): lax.psum(squares.astype(jnp.bfloat16), 'orient').astype(jnp.float32)]
    dot_general x26 -> x0, matrix products: 70.7 us -> none  [the longest x14 58.8 us: batched(): jnp.einsum(spec, left_op, right_op, preferred_element_type=jnp.float32)]
    pmax x1 -> x0, waiting for transfers between devices: 59.4 us -> none  [body(): total_peak = lax.pmax(running_peak, 'orient')]
    pallas_call x0 -> x4, Pallas kernels: none -> 48.1 us  [the longest x1 19.9 us: body(): pl.pallas_call(functools.partial(exchange_kernel, n_tile, n_orient), out_...]
    convert_element_type x6 -> x1, other arithmetic: 27.8 us -> 2.8 us  [body(): return (both[0].astype(f32), both[1].astype(f32))]
    reduce_sum x2 -> x0, other arithmetic: 11.9 us -> none  [the longest x1 9.79 us: correlate(): jnp.mean(filt_real * filt_real + filt_imag * filt_imag, axis=(1, 2), keep...]
    add x2 -> x0, local copies, waits for them, and re-layouts: 5.21 us -> none  [template_spectrum(): jnp.dot(col_cos, tpl_real, preferred_element_type=jnp.float32)]
    mul x4 -> x0, other arithmetic: 4.83 us -> none  [the longest x1 3 us: finish_scores(): (running_peak - mean_score) * lax.rsqrt(variance + 1e-06)]
  transfers between devices with their start and end apart: 4 -> 0, of which waited for: 4 -> 0; matrix products, arithmetic and copies ran while one was open for 21% -> 0% of each run, Pallas kernels for 0% -> 0%
where the time goes in v1:
time: 51.8 us; the launch traced here: 51.5 us
  Pallas kernels  48.1 us (93%)
  other arithmetic  2.8 us (5%)
  between operations  0.65 us (1%)
    pallas_call x1, Pallas kernels, body(): pl.pallas_call(functools.partial(exchange_kernel, n_tile, n_orient), out_...  19.9 us
    pallas_call x1, Pallas kernels, body(): pl.pallas_call(functools.partial(search_kernel, tile_count * n_tile), out...  19.7 us
    pallas_call x1, Pallas kernels, body(): pl.pallas_call(forward_kernel, out_shape=(plane, plane, plane, shape((2,...  4.4 us
    pallas_call x1, Pallas kernels, body(): pl.pallas_call(swap_kernel, out_shape=shape((2, 2, VALID, VALID), bf16),...  4.16 us
    convert_element_type x1, other arithmetic, body(): return (both[0].astype(f32), both[1].astype(f32))  2.8 us

profile of v1, /device:TPU:0, one launch (start us, length us, event | category | flops | bytes accessed | tf_op | source)
XLA Modules:
  0.0 51.5 jit_solution(11806500339440216830)
XLA Ops:
  0.6 4.4 %shard_map.149 = (f32[272,512]{1,0:T(8,128)}, f32[272,512]{1,0:T(8,128)}, f32[272,512]{1,0:T(8,128)}, bf16[2,272,256]{2,1,0:T(8,128)(2,1)}, bf16[2,128,128]{2,1,0:T(8,128)(2,1)}) custom-call(s32[1,2]{1,0:T(1,128)} %ids_ref.1, s32[2,2]{1,0:T(2,128)} %off_ref.1, bf16[2,512,512]{2,1,0:T(8,128)(2,1)} %x_ref.1, bf16[8,1,128,128]{3,2,1,0:T(8,128)(2,1)} %lib_ref.1, ...), custom_call_target="tpu_custom_call" | custom-call | tf_op jit(solution)/shard_map/pallas_call | solution.py:299
  5.0 19.9 %shard_map.150 = (f32[2,272,256]{2,1,0:T(8,128)}, bf16[2,4,2,128,128]{4,3,2,1,0:T(8,128)(2,1)}) custom-call(bf16[2,272,256]{2,1,0:T(8,128)(2,1)} %get-tuple-element.12.pow_ref, bf16[2,128,128]{2,1,0:T(8,128)(2,1)} %get-tuple-element.13.tpl_ref), custom_call_target="tpu_custom_call" | custom-call | tf_op jit(solution)/shard_map/pallas_call | solution.py:311
  24.9 19.7 %shard_map.151.in_ref = bf16[2,384,384]{2,1,0:T(8,128)(2,1)} custom-call(f32[272,512]{1,0:T(8,128)} %get-tuple-element.9.real_ref, f32[272,512]{1,0:T(8,128)} %get-tuple-element.10.imag_ref, f32[272,512]{1,0:T(8,128)} %get-tuple-element.11.con_ref, f32[2,272,256]{2,1,0:T(8,128)} %get-tuple-element.14.total_ref, bf16[8,2,128,128]{3,2,1,0:T(8,128)(2,1)} %bitcast.7, ...), custom_call_target="tpu_custom_call" | custom-call | tf_op jit(solution)/shard_map/pallas_call | solution.py:330
  44.6 4.2 %shard_map.152 = bf16[2,2,384,384]{3,2,1,0:T(8,128)(2,1)} custom-call(bf16[2,384,384]{2,1,0:T(8,128)(2,1)} %shard_map.151.in_ref), custom_call_target="tpu_custom_call" | custom-call | tf_op jit(solution)/shard_map/pallas_call | solution.py:352
  48.7 2.8 %bitcast_convert_fusion = (f32[2,384,384]{2,1,0:T(8,128)}, f32[2,384,384]{2,1,0:T(8,128)}) fusion(bf16[2,2,384,384]{3,2,1,0:T(8,128)(2,1)} %shard_map.152), kind=kLoop, calls=%fused_computation | loop fusion | flops 589824 | bytes 3538944 | tf_op jit(solution)/shard_map/convert_element_type | solution.py:364

commit v2 on v1

--- a/solution.py
+++ b/solution.py
@@ -94,28 +94,85 @@
     return angle * poly
 
 
-def forward_kernel(
+def opening_kernel(
+    n_tile, n_orient,
     ids_ref, off_ref, x_ref, lib_ref, first_ref, cos_ref, sin_ref, a_ref, b_ref,
-    real_ref, imag_ref, con_ref, pow_ref, tpl_ref,
+    real_ref, imag_ref, con_ref, total_ref, all_ref,
+    power, pair_in, sum_out, sum_in, done_out, done_in, pick_out, pick_in, held,
+    send_sem, recv_sem,
 ):
-    core = lax.rem(lax.axis_index("orient"), 2)
-    mine = lax.axis_index("tile")
-    slots = lib_ref.shape[0]
+    tile = lax.axis_index("tile")
+    orient = lax.axis_index("orient")
+    core = lax.rem(orient, 2)
+    chip = orient // 2
+    n_chip = n_orient // 2
+    bits = n_tile.bit_length() - 1
     rows, length = real_ref.shape
     half = length // 2
-    for step in range(tpl_ref.shape[0]):
+    slots = lib_ref.shape[0]
+    steps = pick_out.shape[1]
+    partner = (tile, chip * 2 + 1 - core)
+    across = []
+    for bit in range(bits):
+        side = lax.rem(tile // (1 << bit), 2)
+        across.append((tile + (1 - 2 * side) * (1 << bit), orient))
+    chips = [(tile, lax.rem(chip + k, n_chip) * 2 + core) for k in range(1, n_chip)]
+
+    barrier = pltpu.get_barrier_semaphore()
+    for device in [partner] + across + chips:
+        pl.semaphore_signal(barrier, inc=1, device_id=device, device_id_type=MESH)
+
+    used = [0]
+
+    def send(src, dst, device):
+        at = used[0]
+        used[0] += 1
+        copy = pltpu.make_async_remote_copy(
+            src_ref=src, dst_ref=dst, send_sem=send_sem.at[at], recv_sem=recv_sem.at[at],
+            device_id=device, device_id_type=MESH,
+        )
+        copy.start()
+        return copy
+
+    for step in range(steps):
         chosen = ids_ref[0, step]
         owner = chosen // slots
         picked = lib_ref[chosen - owner * slots, 0]
-        keep = jnp.where(owner == mine, 1.0, 0.0).astype(jnp.float32)
-        tpl_ref[step] = jnp.where(keep > 0.0, picked.astype(jnp.float32), 0.0).astype(jnp.bfloat16)
+        keep = jnp.where(owner == tile, 1.0, 0.0).astype(jnp.float32)
+        pick_out[0, step] = jnp.where(keep > 0.0, picked.astype(jnp.float32), 0.0).astype(jnp.bfloat16)
+    pl.semaphore_wait(barrier, 1 + len(across) + len(chips))
+
+    def start_picks(stage):
+        return [
+            send(pick_out.at[stage, step], pick_in.at[stage, step], across[(stage + step) % bits])
+            for step in range(steps)
+        ]
+
+    def end_picks(stage, copies):
+        for step, copy in enumerate(copies):
+            copy.wait()
+            value = pick_out[stage, step].astype(jnp.float32) + pick_in[stage, step].astype(jnp.float32)
+            if stage + 1 < bits:
+                pick_out[stage + 1, step] = value.astype(jnp.bfloat16)
+            else:
+                held[core, chip, step] = value.astype(jnp.bfloat16)
+
+    picks = start_picks(0)
     halves = dot_nt(first_ref[...], x_ref[core]).astype(jnp.bfloat16)
     half_real, half_imag = halves[:rows], halves[rows:]
-    spec_real = dot(half_real, cos_ref[...]) + dot(half_imag, sin_ref[...])
+    for stage in range(bits):
+        end_picks(stage, picks)
+        if stage + 1 < bits:
+            picks = start_picks(stage + 1)
+        if stage == 0:
+            spec_real = dot(half_real, cos_ref[...]) + dot(half_imag, sin_ref[...])
+    spread = [send(held.at[core, chip], held.at[core, chip], device) for device in chips]
     spec_imag = dot(half_imag, cos_ref[...]) - dot(half_real, sin_ref[...])
-    power = spec_real * spec_real + spec_imag * spec_imag
-    pow_ref[0] = power[:, :half].astype(jnp.bfloat16)
-    pow_ref[1] = power[:, half:].astype(jnp.bfloat16)
+    value = spec_real * spec_real + spec_imag * spec_imag
+    power[0] = value[:, :half].astype(jnp.bfloat16)
+    power[1] = value[:, half:].astype(jnp.bfloat16)
+    pair = send(power.at[1 - core], pair_in, partner)
+
     s2 = a_ref[...] + b_ref[...]
     tilt = (off_ref[core, 0] - off_ref[core, 1]).astype(jnp.float32)
     defocus = DEFOCUS_BASE + DEFOCUS_TILT * tilt
@@ -126,60 +183,29 @@
     real_ref[...] = spec_real * contrast
     imag_ref[...] = spec_imag * contrast
 
-
-def exchange_kernel(
-    n_tile, n_orient, pow_ref, tpl_ref, total_ref, all_ref,
-    pair_in, half_out, half_in, done_out, done_in, tpl_in, held, send_sem, recv_sem,
-):
-    tile = lax.axis_index("tile")
-    orient = lax.axis_index("orient")
-    core = lax.rem(orient, 2)
-    chip = orient // 2
-    n_chip = n_orient // 2
-    partner = (tile, chip * 2 + 1 - core)
-    tiles = [(lax.rem(tile + k, n_tile), orient) for k in range(1, n_tile)]
-    chips = [(tile, lax.rem(chip + k, n_chip) * 2 + core) for k in range(1, n_chip)]
-
-    barrier = pltpu.get_barrier_semaphore()
-    for device in [partner] + tiles + chips:
-        pl.semaphore_signal(barrier, inc=1, device_id=device, device_id_type=MESH)
-    pl.semaphore_wait(barrier, 1 + len(tiles) + len(chips))
-
-    used = [0]
-
-    def send(src, dst, device):
-        at = used[0]
-        used[0] += 1
-        copy = pltpu.make_async_remote_copy(
-            src_ref=src, dst_ref=dst, send_sem=send_sem.at[at], recv_sem=recv_sem.at[at],
-            device_id=device, device_id_type=MESH,
-        )
-        copy.start()
-        return copy
-
-    pair = send(pow_ref.at[1 - core], pair_in, partner)
-    picks = [send(tpl_ref, tpl_in.at[k], device) for k, device in enumerate(tiles)]
     pair.wait()
-    mine = pow_ref[core].astype(jnp.float32) + pair_in[...].astype(jnp.float32)
-    half_out[...] = mine.astype(jnp.bfloat16)
-    sums = [send(half_out, half_in.at[k], device) for k, device in enumerate(tiles)]
-    template = tpl_ref[...].astype(jnp.float32)
-    for k, copy in enumerate(picks):
-        copy.wait()
-        template = template + tpl_in[k].astype(jnp.float32)
-    held[core, chip] = template.astype(jnp.bfloat16)
-    spread = [send(held.at[core, chip], held.at[core, chip], device) for device in chips]
-    for copy in sums:
-        copy.wait()
-    total = half_out[...].astype(jnp.float32)
-    for k in range(len(tiles)):
-        total = total + half_in[k].astype(jnp.float32)
+    total = power[core].astype(jnp.float32) + pair_in[...].astype(jnp.float32)
+    quarter = half // 2
+    for stage in range(bits):
+        sum_out[stage, 0] = total[:, :quarter].astype(jnp.bfloat16)
+        sum_out[stage, 1] = total[:, quarter:].astype(jnp.bfloat16)
+        copies = [
+            send(sum_out.at[stage, piece], sum_in.at[stage, piece], across[(stage + piece) % bits])
+            for piece in range(2)
+        ]
+        parts = []
+        for piece, copy in enumerate(copies):
+            copy.wait()
+            parts.append(
+                sum_out[stage, piece].astype(jnp.float32) + sum_in[stage, piece].astype(jnp.float32)
+            )
+        total = jnp.concatenate(parts, axis=1)
     done_out[...] = total
     last = send(done_out, done_in, partner)
+    total_ref[core] = total
     for copy in spread:
         copy.wait()
     swap = send(held.at[core], held.at[core], partner)
-    total_ref[core] = total
     last.wait()
     total_ref[1 - core] = done_in[...]
     swap.wait()
@@ -287,7 +313,7 @@
     slots, _, size, _ = library.shape
     steps = orient_ids.shape[1]
     n_chip = n_orient // 2
-    assert tile_count == 2 and n_orient % 2 == 0
+    assert tile_count == 2 and n_orient % 2 == 0 and n_tile & (n_tile - 1) == 0
     half = length // 2
     t = tables(length, VALID)
     rows = t["weight"].shape[0]
@@ -296,36 +322,35 @@
     plane = shape((rows, length), f32)
     params = pltpu.CompilerParams(vmem_limit_bytes=GRANT)
 
-    real, imag, contrast, power, picked = pl.pallas_call(
-        forward_kernel,
-        out_shape=(plane, plane, plane, shape((2, rows, half), bf16), shape((steps, size, size), bf16)),
+    bits = n_tile.bit_length() - 1
+    copies = 3 + bits * (steps + 2) + (n_chip - 1)
+    real, imag, contrast, total, templates = pl.pallas_call(
+        functools.partial(opening_kernel, n_tile, n_orient),
+        out_shape=(
+            plane, plane, plane, shape((2, rows, half), f32), shape((2, n_chip, steps, size, size), bf16)
+        ),
         in_specs=[SMEM, SMEM] + [VMEM] * 7,
         out_specs=(VMEM,) * 5,
-        compiler_params=params,
-    )(
-        orient_ids, tile_offsets, micrograph_tiles, library, t["first"], t["cos"], t["sin"],
-        t["a_square"], t["b_square"],
-    )
-
-    copies = 3 + 2 * (n_tile - 1) + (n_chip - 1)
-    total, templates = pl.pallas_call(
-        functools.partial(exchange_kernel, n_tile, n_orient),
-        out_shape=(shape((2, rows, half), f32), shape((2, n_chip, steps, size, size), bf16)),
-        in_specs=[VMEM] * 2,
-        out_specs=(VMEM,) * 2,
         scratch_shapes=[
+            pltpu.VMEM((2, rows, half), bf16),
             pltpu.VMEM((rows, half), bf16),
-            pltpu.VMEM((rows, half), bf16),
-            pltpu.VMEM((n_tile - 1, rows, half), bf16),
+            pltpu.VMEM((bits, 2, rows, half // 2), bf16),
+            pltpu.VMEM((bits, 2, rows, half // 2), bf16),
             pltpu.VMEM((rows, half), f32),
             pltpu.VMEM((rows, half), f32),
-            pltpu.VMEM((n_tile - 1, steps, size, size), bf16),
+            pltpu.VMEM((bits, steps, size, size), bf16),
+            pltpu.VMEM((bits, steps, size, size), bf16),
             pltpu.VMEM((2, n_chip, steps, size, size), bf16),
             pltpu.SemaphoreType.DMA((copies,)),
             pltpu.SemaphoreType.DMA((copies,)),
         ],
-        compiler_params=pltpu.CompilerParams(collective_id=0, has_side_effects=True),
-    )(power, picked)
+        compiler_params=pltpu.CompilerParams(
+            collective_id=0, has_side_effects=True, vmem_limit_bytes=GRANT
+        ),
+    )(
+        orient_ids, tile_offsets, micrograph_tiles, library, t["first"], t["cos"], t["sin"],
+        t["a_square"], t["b_square"],
+    )
 
     found = pl.pallas_call(
         functools.partial(search_kernel, tile_count * n_tile),

time: 51.8 us -> 53.3 us (1.029)
  Pallas kernels: 48.1 us -> 49.6 us
    pallas_call x2 -> x1, Pallas kernels: 24.2 us -> 25.8 us  [body(): pl.pallas_call(functools.partial(opening_kernel, n_tile, n_orient), out_s...]
where the time goes in v2:
time: 53.3 us; the launch traced here: 53 us
  Pallas kernels  49.6 us (93%)
  other arithmetic  2.8 us (5%)
  between operations  0.65 us (1%)
    pallas_call x1, Pallas kernels, body(): pl.pallas_call(functools.partial(opening_kernel, n_tile, n_orient), out_s...  25.8 us
    pallas_call x1, Pallas kernels, body(): pl.pallas_call(functools.partial(search_kernel, tile_count * n_tile), out...  19.7 us
    pallas_call x1, Pallas kernels, body(): pl.pallas_call(swap_kernel, out_shape=shape((2, 2, VALID, VALID), bf16),...  4.14 us
    convert_element_type x1, other arithmetic, body(): return (both[0].astype(f32), both[1].astype(f32))  2.8 us

profile of v2, /device:TPU:0, one launch (start us, length us, event | category | flops | bytes accessed | tf_op | source)
XLA Modules:
  0.0 53.0 jit_solution(18442033835290335201)
XLA Ops:
  0.6 25.8 %shard_map.149 = (f32[272,512]{1,0:T(8,128)}, f32[272,512]{1,0:T(8,128)}, f32[272,512]{1,0:T(8,128)}, f32[2,272,256]{2,1,0:T(8,128)}, bf16[2,4,2,128,128]{4,3,2,1,0:T(8,128)(2,1)}) custom-call(s32[1,2]{1,0:T(1,128)} %ids_ref.1, s32[2,2]{1,0:T(2,128)} %off_ref.1, bf16[2,512,512]{2,1,0:T(8,128)(2,1)} %x_ref.1, bf16[8,1,128,128]{3,2,1,0:T(8,128)(2,1)} %lib_ref.1, ...), custom_call_target="tpu_custom_call" | custom-call | tf_op jit(solution)/shard_map/pallas_call | solution.py:327
  26.4 19.7 %shard_map.150.in_ref = bf16[2,384,384]{2,1,0:T(8,128)(2,1)} custom-call(f32[272,512]{1,0:T(8,128)} %get-tuple-element.7.real_ref, f32[272,512]{1,0:T(8,128)} %get-tuple-element.8.imag_ref, f32[272,512]{1,0:T(8,128)} %get-tuple-element.9.con_ref, f32[2,272,256]{2,1,0:T(8,128)} %get-tuple-element.10.total_ref, bf16[8,2,128,128]{3,2,1,0:T(8,128)(2,1)} %bitcast.7, ...), custom_call_target="tpu_custom_call" | custom-call | tf_op jit(solution)/shard_map/pallas_call | solution.py:355
  46.1 4.1 %shard_map.151 = bf16[2,2,384,384]{3,2,1,0:T(8,128)(2,1)} custom-call(bf16[2,384,384]{2,1,0:T(8,128)(2,1)} %shard_map.150.in_ref), custom_call_target="tpu_custom_call" | custom-call | tf_op jit(solution)/shard_map/pallas_call | solution.py:377
  50.2 2.8 %bitcast_convert_fusion = (f32[2,384,384]{2,1,0:T(8,128)}, f32[2,384,384]{2,1,0:T(8,128)}) fusion(bf16[2,2,384,384]{3,2,1,0:T(8,128)(2,1)} %shard_map.151), kind=kLoop, calls=%fused_computation | loop fusion | flops 589824 | bytes 3538944 | tf_op jit(solution)/shard_map/convert_element_type | solution.py:389

commit v3 on v1

--- a/solution.py
+++ b/solution.py
@@ -203,8 +203,8 @@
         columns = slice(side * half, (side + 1) * half)
         whiten2 = 1.0 / jnp.maximum(sides[side], floor)
         contrast = con_ref[:, columns]
-        g_real[:, columns] = real_ref[:, columns] * whiten2
-        g_imag[:, columns] = imag_ref[:, columns] * whiten2
+        g_real[:, columns] = (real_ref[:, columns] * whiten2).astype(jnp.bfloat16)
+        g_imag[:, columns] = (imag_ref[:, columns] * whiten2).astype(jnp.bfloat16)
         g_energy[:, columns] = contrast * contrast * whiten2 * (weight / (length * length))
     base_table[:size, :length] = cos_ref[:size]
     base_table[:size, length:] = -sin_ref[:size]
@@ -225,8 +225,9 @@
             base_real, base_imag = base[:, :length], base[:, length:]
             energy = jnp.sum(g_energy[...] * (base_real * base_real + base_imag * base_imag))
             scales.append(lax.rsqrt(energy + 1e-06))
-            prod_real = (g_real[...] * base_real + g_imag[...] * base_imag).astype(jnp.bfloat16)
-            prod_imag = (g_imag[...] * base_real - g_real[...] * base_imag).astype(jnp.bfloat16)
+            short_real, short_imag = base_real.astype(jnp.bfloat16), base_imag.astype(jnp.bfloat16)
+            prod_real = g_real[...] * short_real + g_imag[...] * short_imag
+            prod_imag = g_imag[...] * short_real - g_real[...] * short_imag
             even = dot(
                 jnp.concatenate([prod_real[:, :half], prod_imag[:, :half]], axis=1), even_ref[...]
             )
@@ -333,8 +334,8 @@
         in_specs=[VMEM] * 12,
         out_specs=VMEM,
         scratch_shapes=[
-            pltpu.VMEM((rows, length), f32),
-            pltpu.VMEM((rows, length), f32),
+            pltpu.VMEM((rows, length), bf16),
+            pltpu.VMEM((rows, length), bf16),
             pltpu.VMEM((rows, length), f32),
             pltpu.VMEM((2 * size, 2 * length), bf16),
             pltpu.VMEM((length, steps * VALID), bf16),

time: 51.8 us -> 50.6 us (0.977)
  Pallas kernels: 48.1 us -> 46.9 us
    pallas_call x1, Pallas kernels: 19.7 us -> 18.5 us  [body(): pl.pallas_call(functools.partial(search_kernel, tile_count * n_tile), out...]
where the time goes in v3:
time: 50.6 us; the launch traced here: 50.3 us
  Pallas kernels  46.9 us (93%)
  other arithmetic  2.8 us (6%)
  between operations  0.65 us (1%)
    pallas_call x1, Pallas kernels, body(): pl.pallas_call(functools.partial(exchange_kernel, n_tile, n_orient), out_...  19.9 us
    pallas_call x1, Pallas kernels, body(): pl.pallas_call(functools.partial(search_kernel, tile_count * n_tile), out...  18.5 us
    pallas_call x1, Pallas kernels, body(): pl.pallas_call(forward_kernel, out_shape=(plane, plane, plane, shape((2,...  4.4 us
    pallas_call x1, Pallas kernels, body(): pl.pallas_call(swap_kernel, out_shape=shape((2, 2, VALID, VALID), bf16),...  4.15 us
    convert_element_type x1, other arithmetic, body(): return (both[0].astype(f32), both[1].astype(f32))  2.8 us

profile of v3, /device:TPU:0, one launch (start us, length us, event | category | flops | bytes accessed | tf_op | source)
XLA Modules:
  0.0 50.3 jit_solution(7557509242857608188)
XLA Ops:
  0.6 4.4 %shard_map.149 = (f32[272,512]{1,0:T(8,128)}, f32[272,512]{1,0:T(8,128)}, f32[272,512]{1,0:T(8,128)}, bf16[2,272,256]{2,1,0:T(8,128)(2,1)}, bf16[2,128,128]{2,1,0:T(8,128)(2,1)}) custom-call(s32[1,2]{1,0:T(1,128)} %ids_ref.1, s32[2,2]{1,0:T(2,128)} %off_ref.1, bf16[2,512,512]{2,1,0:T(8,128)(2,1)} %x_ref.1, bf16[8,1,128,128]{3,2,1,0:T(8,128)(2,1)} %lib_ref.1, ...), custom_call_target="tpu_custom_call" | custom-call | tf_op jit(solution)/shard_map/pallas_call | solution.py:300
  5.0 19.9 %shard_map.150 = (f32[2,272,256]{2,1,0:T(8,128)}, bf16[2,4,2,128,128]{4,3,2,1,0:T(8,128)(2,1)}) custom-call(bf16[2,272,256]{2,1,0:T(8,128)(2,1)} %get-tuple-element.12.pow_ref, bf16[2,128,128]{2,1,0:T(8,128)(2,1)} %get-tuple-element.13.tpl_ref), custom_call_target="tpu_custom_call" | custom-call | tf_op jit(solution)/shard_map/pallas_call | solution.py:312
  24.9 18.5 %shard_map.151.in_ref = bf16[2,384,384]{2,1,0:T(8,128)(2,1)} custom-call(f32[272,512]{1,0:T(8,128)} %get-tuple-element.9.real_ref, f32[272,512]{1,0:T(8,128)} %get-tuple-element.10.imag_ref, f32[272,512]{1,0:T(8,128)} %get-tuple-element.11.con_ref, f32[2,272,256]{2,1,0:T(8,128)} %get-tuple-element.14.total_ref, bf16[8,2,128,128]{3,2,1,0:T(8,128)(2,1)} %bitcast.7, ...), custom_call_target="tpu_custom_call" | custom-call | tf_op jit(solution)/shard_map/pallas_call | solution.py:331
  43.4 4.2 %shard_map.152 = bf16[2,2,384,384]{3,2,1,0:T(8,128)(2,1)} custom-call(bf16[2,384,384]{2,1,0:T(8,128)(2,1)} %shard_map.151.in_ref), custom_call_target="tpu_custom_call" | custom-call | tf_op jit(solution)/shard_map/pallas_call | solution.py:353
  47.5 2.8 %bitcast_convert_fusion = (f32[2,384,384]{2,1,0:T(8,128)}, f32[2,384,384]{2,1,0:T(8,128)}) fusion(bf16[2,2,384,384]{3,2,1,0:T(8,128)(2,1)} %shard_map.152), kind=kLoop, calls=%fused_computation | loop fusion | flops 589824 | bytes 3538944 | tf_op jit(solution)/shard_map/convert_element_type | solution.py:365

commit v4 on v3

--- a/solution.py
+++ b/solution.py
@@ -188,8 +188,8 @@
 
 def search_kernel(
     tiles, real_ref, imag_ref, con_ref, total_ref, tpl_ref, first_ref, cos_ref, sin_ref,
-    even_ref, odd_ref, last_ref, weight_ref, out_ref,
-    g_real, g_imag, g_energy, base_table, mids, peak, total_sum, squares,
+    even_ref, odd_ref, last_ref, weight_ref, out_ref, peak_ref, z_ref,
+    wide, copy_sem, g_real, g_imag, g_energy, base_table, mids, peak, total_sum, squares,
 ):
     rows, length = real_ref.shape
     half = length // 2
@@ -259,8 +259,17 @@
     mean_score = total_sum[...] / searched
     variance = squares[...] / searched - mean_score * mean_score
     z_score = (peak[...] - mean_score) * lax.rsqrt(variance + 1e-06)
-    out_ref[0] = peak[...].T.astype(jnp.bfloat16)
-    out_ref[1] = z_score.T.astype(jnp.bfloat16)
+    core = lax.rem(lax.axis_index("orient"), 2)
+    copies = []
+    for which, (value, place) in enumerate(((peak[...], peak_ref), (z_score, z_ref))):
+        short = value.T.astype(jnp.bfloat16)
+        out_ref[which] = short
+        wide[which] = short.astype(jnp.float32)
+        copy = pltpu.make_async_copy(wide.at[which], place.at[core], copy_sem.at[which])
+        copy.start()
+        copies.append(copy)
+    for copy in copies:
+        copy.wait()
 
 
 def swap_kernel(in_ref, out_ref, held, send_sem, recv_sem):
@@ -276,11 +285,8 @@
         device_id=partner, device_id_type=MESH,
     )
     copy.start()
-    for which in range(2):
-        out_ref[which, core] = in_ref[which]
     copy.wait()
-    for which in range(2):
-        out_ref[which, 1 - core] = held[which]
+    out_ref[...] = held[...]
 
 
 def body(n_tile, n_orient, micrograph_tiles, tile_offsets, library, orient_ids):
@@ -328,12 +334,14 @@
         compiler_params=pltpu.CompilerParams(collective_id=0, has_side_effects=True),
     )(power, picked)
 
-    found = pl.pallas_call(
+    found, peak, z_score = pl.pallas_call(
         functools.partial(search_kernel, tile_count * n_tile),
-        out_shape=shape((2, VALID, VALID), bf16),
+        out_shape=(shape((2, VALID, VALID), bf16),) + (shape((2, VALID, VALID), f32),) * 2,
         in_specs=[VMEM] * 12,
-        out_specs=VMEM,
+        out_specs=(VMEM, pl.BlockSpec(memory_space=pl.ANY), pl.BlockSpec(memory_space=pl.ANY)),
         scratch_shapes=[
+            pltpu.VMEM((2, VALID, VALID), f32),
+            pltpu.SemaphoreType.DMA((2,)),
             pltpu.VMEM((rows, length), bf16),
             pltpu.VMEM((rows, length), bf16),
             pltpu.VMEM((rows, length), f32),
@@ -350,9 +358,9 @@
         t["last"], t["weight"],
     )
 
-    both = pl.pallas_call(
+    other = pl.pallas_call(
         swap_kernel,
-        out_shape=shape((2, 2, VALID, VALID), bf16),
+        out_shape=shape((2, VALID, VALID), bf16),
         in_specs=[VMEM],
         out_specs=VMEM,
         scratch_shapes=[
@@ -362,7 +370,11 @@
         ],
         compiler_params=pltpu.CompilerParams(collective_id=1, has_side_effects=True),
     )(found)
-    return (both[0].astype(f32), both[1].astype(f32))
+    place = 1 - lax.axis_index("orient") % 2
+    return tuple(
+        lax.dynamic_update_index_in_dim(whole, other[which].astype(f32), place, 0)
+        for which, whole in enumerate((peak, z_score))
+    )
 
 
 def solution(mesh):

time: 50.6 us -> 51.6 us (1.020)
  local copies, waits for them, and re-layouts: 0 us -> 1.02 us
  other arithmetic: 2.8 us -> 1.95 us
  Pallas kernels: 46.9 us -> 47.7 us
    convert_element_type x1 -> x0, other arithmetic: 2.8 us -> none  [body(): return (both[0].astype(f32), both[1].astype(f32))]
    dynamic_update_slice x0 -> x1, other arithmetic: none -> 1.95 us  [body(): lax.dynamic_update_index_in_dim(whole, other[which].astype(f32), place, 0)]
    unnamed x0 -> x4, local copies, waits for them, and re-layouts: none -> 1.02 us
    pallas_call x1, Pallas kernels: 18.5 us -> 19.5 us  [body(): pl.pallas_call(functools.partial(search_kernel, tile_count * n_tile), out...]
where the time goes in v4:
time: 51.6 us; the launch traced here: 51.4 us
  Pallas kernels  47.7 us (92%)
  other arithmetic  1.95 us (4%)
  local copies, waits for them, and re-layouts  1.02 us (2%)
  between operations  0.69 us (1%)
    pallas_call x1, Pallas kernels, body(): pl.pallas_call(functools.partial(exchange_kernel, n_tile, n_orient), out_...  19.8 us
    pallas_call x1, Pallas kernels, body(): pl.pallas_call(functools.partial(search_kernel, tile_count * n_tile), out...  19.5 us
    pallas_call x1, Pallas kernels, body(): pl.pallas_call(forward_kernel, out_shape=(plane, plane, plane, shape((2,...  4.4 us
    pallas_call x1, Pallas kernels, body(): pl.pallas_call(swap_kernel, out_shape=shape((2, VALID, VALID), bf16), in_...  4.06 us
    dynamic_update_slice x1, other arithmetic, body(): lax.dynamic_update_index_in_dim(whole, other[which].astype(f32), place, 0)  1.95 us

profile of v4, /device:TPU:0, one launch (start us, length us, event | category | flops | bytes accessed | tf_op | source)
XLA Modules:
  0.0 51.4 jit_solution(12511445125354000327)
XLA Ops:
  0.6 4.4 %shard_map.149 = (f32[272,512]{1,0:T(8,128)}, f32[272,512]{1,0:T(8,128)}, f32[272,512]{1,0:T(8,128)}, bf16[2,272,256]{2,1,0:T(8,128)(2,1)}, bf16[2,128,128]{2,1,0:T(8,128)(2,1)}) custom-call(s32[1,2]{1,0:T(1,128)} %ids_ref.1, s32[2,2]{1,0:T(2,128)} %off_ref.1, bf16[2,512,512]{2,1,0:T(8,128)(2,1)} %x_ref.1, bf16[8,1,128,128]{3,2,1,0:T(8,128)(2,1)} %lib_ref.1, ...), custom_call_target="tpu_custom_call" | custom-call | tf_op jit(solution)/shard_map/pallas_call | solution.py:306
  5.0 19.8 %shard_map.150 = (f32[2,272,256]{2,1,0:T(8,128)}, bf16[2,4,2,128,128]{4,3,2,1,0:T(8,128)(2,1)}) custom-call(bf16[2,272,256]{2,1,0:T(8,128)(2,1)} %get-tuple-element.15.pow_ref, bf16[2,128,128]{2,1,0:T(8,128)(2,1)} %get-tuple-element.16.tpl_ref), custom_call_target="tpu_custom_call" | custom-call | tf_op jit(solution)/shard_map/pallas_call | solution.py:318
  24.8 19.5 %shard_map.151 = (bf16[2,384,384]{2,1,0:T(8,128)(2,1)}, f32[2,384,384]{2,1,0:T(8,128)}, f32[2,384,384]{2,1,0:T(8,128)}) custom-call(f32[272,512]{1,0:T(8,128)} %get-tuple-element.12.real_ref, f32[272,512]{1,0:T(8,128)} %get-tuple-element.13.imag_ref, f32[272,512]{1,0:T(8,128)} %get-tuple-element.14.con_ref, f32[2,272,256]{2,1,0:T(8,128)} %get-tuple-element.17.total_ref, ...), custom_call_target="tpu_custom_call" | custom-call | tf_op jit(solution)/shard_map/pallas_call | solution.py:337
  44.3 0.0 copy-start
  44.3 4.1 %shard_map.152 = bf16[2,384,384]{2,1,0:T(8,128)(2,1)} custom-call(bf16[2,384,384]{2,1,0:T(8,128)(2,1)} %get-tuple-element.20.in_ref), custom_call_target="tpu_custom_call" | custom-call | tf_op jit(solution)/shard_map/pallas_call | solution.py:361
  48.4 0.0 copy-done
  48.4 2.0 %convert_dynamic-update-slice_fusion = (f32[2,384,384]{2,1,0:T(8,128)}, f32[2,384,384]{2,1,0:T(8,128)S(1)}) fusion(f32[2,384,384]{2,1,0:T(8,128)} %get-tuple-element.21, s32[]{:T(128)S(6)} %select_n.13, bf16[2,384,384]{2,1,0:T(8,128)(2,1)} %shard_map.152, f32[2,384,384]{2,1,0:T(8,128)S(1)} %copy-done), kind=kLoop, calls=%fused_computation | loop fusion | flops 294912 | bytes 1769476 | tf_op jit(solution)/shard_map/jit(dynamic_update_index_in_dim)/dynamic_update_slice | solution.py:375
  50.4 0.0 copy-start.1
  50.4 1.0 %copy-done.1 = f32[2,384,384]{2,1,0:T(8,128)} copy-done((f32[2,384,384]{2,1,0:T(8,128)}, f32[2,384,384]{2,1,0:T(8,128)S(1)}, u32[]{:S(2)}) %copy-start.1) | copy-done | bytes 1179672
Async XLA Ops:
  44.3 4.1 %copy-start = (f32[2,384,384]{2,1,0:T(8,128)S(1)}, f32[2,384,384]{2,1,0:T(8,128)}, u32[]{:S(2)}) copy-start(f32[2,384,384]{2,1,0:T(8,128)} %get-tuple-element.19) | copy-start | bytes 3538948
  50.4 1.0 %copy-start.1 = (f32[2,384,384]{2,1,0:T(8,128)}, f32[2,384,384]{2,1,0:T(8,128)S(1)}, u32[]{:S(2)}) copy-start(f32[2,384,384]{2,1,0:T(8,128)S(1)} %get-tuple-element.23) | copy-start | bytes 3538948
